TPU v7x, 32 devices: a whole 2x2x4 slice. The times are simulated.
32 devices in a mesh: grp: 2 (over x), pix: 16 (over z, y, core).
Axes of the slice: x: 2, y: 2, z: 4, core: 2. Of those that a mesh axis runs over, the one named last changes fastest.
Arguments:
- particle_images: bfloat16 [8192, 128, 128], P(('grp', 'pix')), parts along dimension 0, may hold values from -6 to 6
- defocus_group: int32 [8192], P(('grp', 'pix')), parts along dimension 0, may hold values from 0 to 63
- live_counts: int32 [32], P(('grp', 'pix')), parts along dimension 0, may hold values from 192 to 256, as said below
- defocus_values: float32 [128], P('grp'), parts along dimension 0, may hold values from 50 to 400
- test_matrix: bfloat16 [32768, 128], P(('grp', 'pix')), parts along dimension 0, may hold values from -0.046875 to 0.046875
Outputs:
- range_basis: bfloat16 [8192, 128], P(('grp', 'pix')), parts along dimension 0
- projection: float32 [32768, 128], P(('grp', 'pix')), parts along dimension 0
There are 2 independent parts, one for each index of `grp`. A program takes and returns all parts, laid end to end along the dimension named above; each array names one. Nothing has to cross between parts.
Inputs may be any that keep to these rules, and one draw needn't show every extreme that they name: `live_counts`: each entry is the number of live particle slots of a shard, counted from its first slot; some shard is full in every draw.
All inputs are finite; a program needn't handle non-finite values.
Results may differ from a plain program's by a relative error of at most 0.011.
Values may be sent and summed in bfloat16 or wider, within the bound.
A program may use at most 192 MiB of HBM per device.

v0:
```python
import math
import jax
import jax.numpy as jnp
from jax import lax
from jax.sharding import PartitionSpec as P

AMPLITUDE = 0.1
WIENER = 0.1


def frequency_sq(length):
    indices = jnp.arange(length, dtype=jnp.int32)
    frequency = (
        jnp.where(indices < length // 2, indices, indices - length).astype(jnp.float32) / length
    )
    return frequency[:, None] ** 2 + frequency[None, :] ** 2


def wiener_table(defocus_values, length):
    phases = jnp.pi * defocus_values[:, None, None] * frequency_sq(length)[None]
    contrast = -(math.sqrt(1.0 - AMPLITUDE**2) * jnp.sin(phases) + AMPLITUDE * jnp.cos(phases))
    return contrast / (contrast * contrast + WIENER)


def dft_tables(length):
    indices = jnp.arange(length, dtype=jnp.int32)
    product = indices[:, None] * indices[None, :] % length
    angles = 2.0 * math.pi / length * product.astype(jnp.float32)
    return (jnp.cos(angles).astype(jnp.bfloat16), jnp.sin(angles).astype(jnp.bfloat16))


def left_apply(table_now, values_now):
    return jnp.einsum("uj,bjv->buv", table_now, values_now, preferred_element_type=jnp.float32)


def right_apply(values_now, table_now):
    return jnp.einsum("bjk,kv->bjv", values_now, table_now, preferred_element_type=jnp.float32)


def correct_block(images_blk, filter_now, cosine_table, sine_table):
    length = cosine_table.shape[0]
    both_tables = jnp.concatenate([cosine_table, sine_table], axis=1)
    first_pass = right_apply(images_blk, both_tables).astype(jnp.bfloat16)
    cos_side = left_apply(cosine_table, first_pass)
    sin_side = left_apply(sine_table, first_pass)
    filt_re = ((cos_side[..., :length] - sin_side[..., length:]) * filter_now).astype(jnp.bfloat16)
    filt_im = (-(cos_side[..., length:] + sin_side[..., :length]) * filter_now).astype(jnp.bfloat16)
    re_both = right_apply(filt_re, both_tables)
    im_both = right_apply(filt_im, both_tables)
    back_re = (re_both[..., :length] - im_both[..., length:]).astype(jnp.bfloat16)
    back_im = (re_both[..., length:] + im_both[..., :length]).astype(jnp.bfloat16)
    result_now = left_apply(cosine_table, back_re) - left_apply(sine_table, back_im)
    return result_now / float(length * length)


def per_device(particle_images, defocus_group, live_counts, defocus_values, test_matrix):
    part_rows = particle_images.shape[0]
    length = particle_images.shape[1]
    pixels = length * length
    groups_all = defocus_values.shape[0]
    filter_table = (
        wiener_table(defocus_values, length).reshape(groups_all, pixels).astype(jnp.bfloat16)
    )
    cosine_table, sine_table = dft_tables(length)
    group_hot = (defocus_group[:, None] == jnp.arange(groups_all, dtype=jnp.int32)[None, :]).astype(
        jnp.bfloat16
    )
    block_size = math.gcd(part_rows, 128)
    blocks = part_rows // block_size

    def correct(block_pair):
        images_blk, hot_blk = block_pair
        filter_now = jnp.dot(hot_blk, filter_table, preferred_element_type=jnp.float32).reshape(
            block_size, length, length
        )
        return correct_block(images_blk, filter_now, cosine_table, sine_table).reshape(
            block_size, pixels
        )

    corrected = lax.map(
        correct,
        (
            particle_images.reshape(blocks, block_size, length, length),
            group_hot.reshape(blocks, block_size, groups_all),
        ),
    )
    corrected = corrected.reshape(part_rows, pixels)
    live_rows = jnp.arange(part_rows, dtype=jnp.int32) < live_counts[0]
    corrected = jnp.where(live_rows[:, None], corrected, 0.0).astype(jnp.bfloat16)
    columns = corrected
    sketch = jnp.dot(
        columns,
        lax.all_gather(test_matrix, "pix", axis=0, tiled=True),
        preferred_element_type=jnp.float32,
    )
    local_gram = jnp.dot(sketch.T, sketch, precision=lax.Precision.HIGHEST)
    factor_low = jnp.linalg.cholesky(lax.psum(local_gram, "pix"))
    range_basis = lax.linalg.triangular_solve(
        factor_low, sketch, left_side=False, lower=True, transpose_a=True
    ).astype(jnp.bfloat16)
    columns = corrected
    projection = lax.psum_scatter(
        lax.dot_general(
            columns, range_basis, (((0,), (0,)), ((), ())), preferred_element_type=jnp.float32
        ),
        "pix",
        scatter_dimension=0,
        tiled=True,
    )
    return (range_basis, projection)


def solution(mesh):
    placed = (
        P(("grp", "pix"), None, None),
        P(("grp", "pix")),
        P(("grp", "pix")),
        P("grp"),
        P(("grp", "pix"), None),
    )
    return jax.shard_map(
        per_device,
        mesh=mesh,
        in_specs=placed,
        out_specs=(P(("grp", "pix"), None), P(("grp", "pix"), None)),
        check_vma=False,
    )
```

profile of v0, /device:TPU:0, one launch (start us, length us, event | category | flops | bytes accessed | tf_op | source)
XLA Modules:
  0.0 487.4 jit_solution(18269629474822703889)
XLA Ops:
  7.2 0.0 all-gather.2.cloned.1.call-start
  7.2 0.7 all-gather.2.cloned.1.call-update
  7.9 0.0 all-reduce.2.cloned.1.call-start
  7.9 0.3 sine_convert_fusion.1
  8.2 0.2 add.82
  8.5 0.7 fusion.82
  9.2 0.7 broadcast_multiply_fusion
  9.8 226.4 %while.13 = (s32[]{:T(128)}, bf16[2,128,16384]{2,1,0:T(8,128)(2,1)}, bf16[2,128,128,128]{3,2,1,0:T(8,128)(2,1)}, bf16[128,256]{1,0:T(8,128)(2,1)S(1)}, bf16[2,12...) while((s32[]{:T(128)}, ...), condition=%wide.region_1.2_spmd.clone.clone, body=%wide.region_0.1_spmd.clone.clone.sunk | while | flops 6754861056 | bytes 285492864 | solution.py:80
  9.8 4.5 convolution_convert_fusion.3
  14.4 7.5 %convolution_bitcast_fusion.4 = f32[128,128,256]{1,2,0:T(8,128)} fusion(bf16[128,128,256]{2,1,0:T(8,128)(2,1)S(1)} %convolution_convert_fusion.3), kind=kOutput, calls=%fused_computation.3.clone.1 | convolution fusion | flops 1073987584 | bytes 25165824 | tf_op jit(solution)/shard_map/while/body/eval_jaxpr/uj,bjv->buv/dot_general | solution.py:33
  21.9 7.3 %convolution_bitcast_fusion.5 = f32[128,128,256]{1,2,0:T(8,128)} fusion(bf16[128,128,256]{2,1,0:T(8,128)(2,1)S(1)} %convolution_convert_fusion.3), kind=kOutput, calls=%fused_computation.4.clone.1 | convolution fusion | flops 1073987584 | bytes 25165824 | tf_op jit(solution)/shard_map/while/body/eval_jaxpr/uj,bjv->buv/dot_general | solution.py:33
  29.1 18.8 %fusion.138 = f32[128,128,128]{2,0,1:T(8,128)} fusion(bf16[2,128,64]{1,2,0:T(8,128)(2,1)S(1)} %get-tuple-element.202, s32[]{:T(128)} %get-tuple-element.190, f32[16384]{0:T(1024)S(1)} %get-tuple-element.203, f32[64]{0:T(128)S(1)} %get-tuple-element.204), kind=kOutput, calls=%fused_computation.35.clone.1 | convolution fusion | flops 277872640 | bytes 8471044 | tf_op jit(solution)/shard_map/while/body/eval_jaxpr/dot_general | solution.py:73
  48.0 9.4 %copy.62 = f32[128,128,128]{1,2,0:T(8,128)} copy(f32[128,128,128]{2,0,1:T(8,128)} %fusion.138) | data formatting | bytes 16777216 | tf_op jit(solution)/shard_map/while/body/eval_jaxpr/dot_general | solution.py:73
  57.3 16.7 %fusion.140 = f32[128,128,256]{2,1,0:T(8,128)} fusion(f32[128,128,128]{1,2,0:T(8,128)} %copy.62, f32[128,128,256]{1,2,0:T(8,128)} %convolution_bitcast_fusion.4, f32[128,128,256]{1,2,0:T(8,128)} %convolution_bitcast_fusion.5, bf16[128,256]{1,0:T(8,128)(2,1)S(1)} %get-tuple-element.201), kind=kOutput, calls=%fused_computation.28.clone.1 | convolution fusion | flops 1080033280 | bytes 42008576 | tf_op jit(solution)/shard_map/while/body/eval_jaxpr/bjk,kv->bjv/dot_general | solution.py:37
  74.0 14.0 %fusion.139 = f32[128,128,256]{2,1,0:T(8,128)} fusion(f32[128,128,128]{1,2,0:T(8,128)S(1)} %copy-done, f32[128,128,256]{1,2,0:T(8,128)} %convolution_bitcast_fusion.4, f32[128,128,256]{1,2,0:T(8,128)} %convolution_bitcast_fusion.5, bf16[128,256]{1,0:T(8,128)(2,1)S(1)} %get-tuple-element.201), kind=kOutput, calls=%fused_computation.29.clone.1 | convolution fusion | flops 1082130432 | bytes 42008576 | tf_op jit(solution)/shard_map/while/body/eval_jaxpr/bjk,kv->bjv/dot_general | solution.py:37
  88.0 7.5 %fusion.141 = f32[128,128,128]{2,1,0:T(8,128)S(1)} fusion(f32[128,128,256]{2,1,0:T(8,128)} %fusion.139, f32[128,128,256]{2,1,0:T(8,128)} %fusion.140), kind=kOutput, calls=%fused_computation.30.clone.1 | convolution fusion | flops 541310976 | bytes 25165824 | tf_op jit(solution)/shard_map/while/body/eval_jaxpr/uj,bjv->buv/dot_general | solution.py:33
  95.5 9.7 %multiply_bitcast_fusion.2 = bf16[128,128,128]{1,2,0:T(8,128)(2,1)} fusion(f32[128,128,128]{2,1,0:T(8,128)S(1)} %fusion.141, f32[128,128,256]{2,1,0:T(8,128)} %fusion.139, f32[128,128,256]{2,1,0:T(8,128)} %fusion.140), kind=kOutput, calls=%fused_computation.16.clone.1 | convolution fusion | flops 547602432 | bytes 29360128 | tf_op jit(solution)/shard_map/while/body/eval_jaxpr/uj,bjv->buv/dot_general | solution.py:33
  105.2 7.3 %copy.63 = bf16[128,128,128]{0,2,1:T(8,128)(2,1)} copy(bf16[128,128,128]{1,2,0:T(8,128)(2,1)} %multiply_bitcast_fusion.2) | data formatting | bytes 8388608 | tf_op jit(solution)/shard_map/while/body/eval_jaxpr/div | solution.py:53
  112.5 6.4 %copy.64 = bf16[1,128,16384]{2,1,0:T(8,128)(2,1)} copy(bf16[1,128,16384]{1,2,0:T(8,128)(2,1)} %bitcast.100) | data formatting | bytes 8388608 | tf_op jit(solution)/shard_map/while/body/jit(dynamic_update_index_in_dim)/dynamic_update_slice | solution.py:80
  118.8 4.5 constant_dynamic-update-slice_fusion.2
  123.4 4.5 convolution_convert_fusion.3
  127.9 7.3 %convolution_bitcast_fusion.4 = f32[128,128,256]{1,2,0:T(8,128)} fusion(bf16[128,128,256]{2,1,0:T(8,128)(2,1)S(1)} %convolution_convert_fusion.3), kind=kOutput, calls=%fused_computation.3.clone.1 | convolution fusion | flops 1073987584 | bytes 25165824 | tf_op jit(solution)/shard_map/while/body/eval_jaxpr/uj,bjv->buv/dot_general | solution.py:33
  135.1 7.2 %convolution_bitcast_fusion.5 = f32[128,128,256]{1,2,0:T(8,128)} fusion(bf16[128,128,256]{2,1,0:T(8,128)(2,1)S(1)} %convolution_convert_fusion.3), kind=kOutput, calls=%fused_computation.4.clone.1 | convolution fusion | flops 1073987584 | bytes 25165824 | tf_op jit(solution)/shard_map/while/body/eval_jaxpr/uj,bjv->buv/dot_general | solution.py:33
  142.4 18.8 %fusion.138 = f32[128,128,128]{2,0,1:T(8,128)} fusion(bf16[2,128,64]{1,2,0:T(8,128)(2,1)S(1)} %get-tuple-element.202, s32[]{:T(128)} %get-tuple-element.190, f32[16384]{0:T(1024)S(1)} %get-tuple-element.203, f32[64]{0:T(128)S(1)} %get-tuple-element.204), kind=kOutput, calls=%fused_computation.35.clone.1 | convolution fusion | flops 277872640 | bytes 8471044 | tf_op jit(solution)/shard_map/while/body/eval_jaxpr/dot_general | solution.py:73
  161.2 9.3 %copy.62 = f32[128,128,128]{1,2,0:T(8,128)} copy(f32[128,128,128]{2,0,1:T(8,128)} %fusion.138) | data formatting | bytes 16777216 | tf_op jit(solution)/shard_map/while/body/eval_jaxpr/dot_general | solution.py:73
  170.5 16.4 %fusion.140 = f32[128,128,256]{2,1,0:T(8,128)} fusion(f32[128,128,128]{1,2,0:T(8,128)} %copy.62, f32[128,128,256]{1,2,0:T(8,128)} %convolution_bitcast_fusion.4, f32[128,128,256]{1,2,0:T(8,128)} %convolution_bitcast_fusion.5, bf16[128,256]{1,0:T(8,128)(2,1)S(1)} %get-tuple-element.201), kind=kOutput, calls=%fused_computation.28.clone.1 | convolution fusion | flops 1080033280 | bytes 42008576 | tf_op jit(solution)/shard_map/while/body/eval_jaxpr/bjk,kv->bjv/dot_general | solution.py:37
  186.9 14.0 %fusion.139 = f32[128,128,256]{2,1,0:T(8,128)} fusion(f32[128,128,128]{1,2,0:T(8,128)S(1)} %copy-done, f32[128,128,256]{1,2,0:T(8,128)} %convolution_bitcast_fusion.4, f32[128,128,256]{1,2,0:T(8,128)} %convolution_bitcast_fusion.5, bf16[128,256]{1,0:T(8,128)(2,1)S(1)} %get-tuple-element.201), kind=kOutput, calls=%fused_computation.29.clone.1 | convolution fusion | flops 1082130432 | bytes 42008576 | tf_op jit(solution)/shard_map/while/body/eval_jaxpr/bjk,kv->bjv/dot_general | solution.py:37
  200.9 7.5 %fusion.141 = f32[128,128,128]{2,1,0:T(8,128)S(1)} fusion(f32[128,128,256]{2,1,0:T(8,128)} %fusion.139, f32[128,128,256]{2,1,0:T(8,128)} %fusion.140), kind=kOutput, calls=%fused_computation.30.clone.1 | convolution fusion | flops 541310976 | bytes 25165824 | tf_op jit(solution)/shard_map/while/body/eval_jaxpr/uj,bjv->buv/dot_general | solution.py:33
  208.4 9.7 %multiply_bitcast_fusion.2 = bf16[128,128,128]{1,2,0:T(8,128)(2,1)} fusion(f32[128,128,128]{2,1,0:T(8,128)S(1)} %fusion.141, f32[128,128,256]{2,1,0:T(8,128)} %fusion.139, f32[128,128,256]{2,1,0:T(8,128)} %fusion.140), kind=kOutput, calls=%fused_computation.16.clone.1 | convolution fusion | flops 547602432 | bytes 29360128 | tf_op jit(solution)/shard_map/while/body/eval_jaxpr/uj,bjv->buv/dot_general | solution.py:33
  218.1 7.3 %copy.63 = bf16[128,128,128]{0,2,1:T(8,128)(2,1)} copy(bf16[128,128,128]{1,2,0:T(8,128)(2,1)} %multiply_bitcast_fusion.2) | data formatting | bytes 8388608 | tf_op jit(solution)/shard_map/while/body/eval_jaxpr/div | solution.py:53
  225.3 6.4 %copy.64 = bf16[1,128,16384]{2,1,0:T(8,128)(2,1)} copy(bf16[1,128,16384]{1,2,0:T(8,128)(2,1)} %bitcast.100) | data formatting | bytes 8388608 | tf_op jit(solution)/shard_map/while/body/jit(dynamic_update_index_in_dim)/dynamic_update_slice | solution.py:80
  231.7 4.5 constant_dynamic-update-slice_fusion.2
  236.9 8.6 %fusion.72 = bf16[256,16384]{1,0:T(8,128)(2,1)} fusion(bf16[2,128,16384]{2,1,0:T(8,128)(2,1)} %get-tuple-element.79, pred[256]{0:T(512)(128)(4,1)S(1)} %iota_compare_fusion.3), kind=kLoop, calls=%fused_computation.76 | loop fusion | flops 4194304 | bytes 16777472 | tf_op jit(solution)/shard_map/convert_element_type | solution.py:89
  245.4 6.9 %fusion.86 = f32[256,128]{1,0:T(8,128)S(1)} fusion(bf16[256,16384]{1,0:T(8,128)(2,1)} %fusion.72, bf16[16384,128]{1,0:T(8,128)(2,1)} %all-gather.2.cloned.1.call-done), kind=kOutput, calls=%fused_computation.108 | convolution fusion | flops 1073741824 | bytes 12713984 | tf_op jit(solution)/shard_map/dot_general | solution.py:91
  252.4 1.0 fusion.87
  253.4 0.0 all-reduce.2.cloned.1.call-update
  253.4 0.0 reduce-scatter.2.cloned.1.call-start
  253.4 87.1 %all-reduce.2.cloned.1.call-done = f32[128,128]{0,1:T(8,128)} async-done(((f32[128,128]{0,1:T(8,128)}), f32[128,128]{0,1:T(8,128)}) %all-reduce.2.cloned.1.call-update) | async-done | bytes 65552 | tf_op jit(solution)/shard_map/psum | solution.py:97
  340.6 0.9 copy.41
  341.5 0.9 fusion.78
  342.3 11.7 %cholesky.16 = f32[128,128]{1,0:T(8,128)S(1)} custom-call(f32[128,128]{1,0:T(8,128)S(1)} %fusion.78), custom_call_target="Cholesky" | custom-call | tf_op jit(solution)/shard_map/jit(cholesky)/cholesky | solution.py:97
  354.1 0.6 compare_reduce_fusion
  354.7 0.7 fusion.73
  355.4 9.8 %custom-call.6 = f32[1,128,128]{1,2,0:T(8,128)S(1)} custom-call(f32[1,128,128]{2,1,0:T(8,128)S(1)} %fusion.73), custom_call_target="InvertDiagBlocksLowerTriangular" | custom-call | tf_op jit(solution)/shard_map/triangular_solve | solution.py:98
  365.2 0.3 convolution_convert_fusion.1
  365.5 9.0 %fusion.88 = f32[16384,128]{1,0:T(8,128)} fusion(bf16[256,16384]{1,0:T(8,128)(2,1)} %fusion.72, bf16[256,128]{1,0:T(8,128)(2,1)S(1)} %convolution_convert_fusion.1), kind=kOutput, calls=%fused_computation.110 | convolution fusion | flops 1073741824 | bytes 16842752 | tf_op jit(solution)/shard_map/dot_general | solution.py:103
  374.5 0.0 reduce-scatter.2.cloned.1.call-update
  374.6 106.3 %reduce-scatter.2.cloned.1.call-done = f32[1024,128]{1,0:T(8,128)} async-done(((f32[16384,128]{1,0:T(8,128)}), f32[1024,128]{1,0:T(8,128)}) %reduce-scatter.2.cloned.1.call-update) | async-done | bytes 524304 | tf_op jit(solution)/shard_map/reduce_scatter | solution.py:102
  (13 shorter events, 0.1 us)
Async XLA Ops:
  7.2 238.3 %all-gather.2.cloned.1.call-start = ((), (), s32[]{:S(2)}) async-start(), calls=%async_computation.1 | async-start | bytes 4456448 | tf_op jit(solution)/shard_map/all_gather | solution.py:93
  7.9 332.7 %all-reduce.2.cloned.1.call-start = ((), (), s32[]{:S(2)}) async-start(), calls=%async_computation.2 | async-start | bytes 131072 | tf_op jit(solution)/shard_map/psum | solution.py:97
  57.3 16.7 %copy-start = (f32[128,128,128]{1,2,0:T(8,128)S(1)}, f32[128,128,128]{1,2,0:T(8,128)}, u32[]{:S(2)}) copy-start(f32[128,128,128]{1,2,0:T(8,128)} %copy.62) | copy-start | bytes 25165828 | tf_op jit(solution)/shard_map/while
  170.5 16.4 %copy-start = (f32[128,128,128]{1,2,0:T(8,128)S(1)}, f32[128,128,128]{1,2,0:T(8,128)}, u32[]{:S(2)}) copy-start(f32[128,128,128]{1,2,0:T(8,128)} %copy.62) | copy-start | bytes 25165828 | tf_op jit(solution)/shard_map/while
  253.4 227.5 %reduce-scatter.2.cloned.1.call-start = ((), (), s32[]{:S(2)}) async-start(), calls=%async_computation.3 | async-start | bytes 8912896 | tf_op jit(solution)/shard_map/reduce_scatter | solution.py:102
  365.5 9.1 %copy-start.1 = (bf16[256,128]{1,0:T(8,128)(2,1)}, bf16[256,128]{1,0:T(8,128)(2,1)S(1)}, u32[]{:S(2)}) copy-start(bf16[256,128]{1,0:T(8,128)(2,1)S(1)} %convolution_convert_fusion.1) | copy-start | bytes 196612
Sparse Core Ops, SparseCore 0:
  10.2 53.3 all-gather.1
  253.5 86.9 all-reduce.1
  374.7 106.1 reduce-scatter.1
where the time goes:
time: 489 us; the launch traced here: 487 us
  waiting for transfers between devices  194 us (40%)
  matrix products  189 us (39%)
  local copies, waits for them, and re-layouts  56.1 us (11%)
  other arithmetic  34 us (7%)
  between operations  14.5 us (3%)
    reduce_scatter x1, waiting for transfers between devices, per_device(): lax.psum_scatter(lax.dot_general(columns, range_basis, (((0,), (0,)), (()...  106 us
    psum x1, waiting for transfers between devices, per_device(): factor_low = jnp.linalg.cholesky(lax.psum(local_gram, 'pix'))  87.1 us
    dot_general x6, matrix products, right_apply(): jnp.einsum('bjk,kv->bjv', values_now, table_now, preferred_element_type=j...  70.1 us
    dot_general x8, matrix products, left_apply(): jnp.einsum('uj,bjv->buv', table_now, values_now, preferred_element_type=j...  63.6 us
    dot_general x2, matrix products, correct(): jnp.dot(hot_blk, filter_table, preferred_element_type=jnp.float32)  37.7 us
    dynamic_update_slice x4, local copies, waits for them, and re-layouts, per_device(): lax.map(correct, (particle_images.reshape(blocks, block_size, length, len...  21.7 us
    dot_general x2, local copies, waits for them, and re-layouts, correct(): jnp.dot(hot_blk, filter_table, preferred_element_type=jnp.float32)  18.6 us
    div x2, local copies, waits for them, and re-layouts, correct_block(): return result_now / float(length * length)  14.5 us
  transfers between devices with their start and end apart: 3, of which 2 were waited for; matrix products, arithmetic and copies ran while one was open for 49% of the time, Pallas kernels for 0%

commit v1 on v0

--- a/solution.py
+++ b/solution.py
@@ -94,7 +94,7 @@
         preferred_element_type=jnp.float32,
     )
     local_gram = jnp.dot(sketch.T, sketch, precision=lax.Precision.HIGHEST)
-    factor_low = jnp.linalg.cholesky(lax.psum(local_gram, "pix"))
+    factor_low = jnp.linalg.cholesky(jnp.sum(lax.all_gather(local_gram, "pix"), axis=0))
     range_basis = lax.linalg.triangular_solve(
         factor_low, sketch, left_side=False, lower=True, transpose_a=True
     ).astype(jnp.bfloat16)

time: 489 us -> 439 us (0.90)
  waiting for transfers between devices: 194 us -> 145 us
    psum x1 -> x0, waiting for transfers between devices: 87.1 us -> none  [per_device(): factor_low = jnp.linalg.cholesky(lax.psum(local_gram, 'pix'))]
    all_gather x0 -> x1, waiting for transfers between devices: none -> 40.6 us  [per_device(): lax.all_gather(local_gram, 'pix')]
  transfers between devices with their start and end apart: 3 -> 3, of which waited for: 2 -> 2; matrix products, arithmetic and copies ran while one was open for 49% -> 54% of each run, Pallas kernels for 0% -> 0%
where the time goes in v1:
time: 439 us; the launch traced here: 438 us
  matrix products  189 us (43%)
  waiting for transfers between devices  145 us (33%)
  local copies, waits for them, and re-layouts  55.2 us (13%)
  other arithmetic  34.4 us (8%)
  between operations  14.5 us (3%)
    reduce_scatter x1, waiting for transfers between devices, per_device(): lax.psum_scatter(lax.dot_general(columns, range_basis, (((0,), (0,)), (()...  104 us
    dot_general x6, matrix products, right_apply(): jnp.einsum('bjk,kv->bjv', values_now, table_now, preferred_element_type=j...  70.1 us
    dot_general x8, matrix products, left_apply(): jnp.einsum('uj,bjv->buv', table_now, values_now, preferred_element_type=j...  63.6 us
    all_gather x1, waiting for transfers between devices, per_device(): lax.all_gather(local_gram, 'pix')  40.6 us
    dot_general x2, matrix products, correct(): jnp.dot(hot_blk, filter_table, preferred_element_type=jnp.float32)  37.7 us
    dynamic_update_slice x4, local copies, waits for them, and re-layouts, per_device(): lax.map(correct, (particle_images.reshape(blocks, block_size, length, len...  21.7 us
    dot_general x2, local copies, waits for them, and re-layouts, correct(): jnp.dot(hot_blk, filter_table, preferred_element_type=jnp.float32)  18.6 us
    div x2, local copies, waits for them, and re-layouts, correct_block(): return result_now / float(length * length)  14.5 us
  transfers between devices with their start and end apart: 3, of which 2 were waited for; matrix products, arithmetic and copies ran while one was open for 54% of the time, Pallas kernels for 0%

profile of v1, /device:TPU:0, one launch (start us, length us, event | category | flops | bytes accessed | tf_op | source)
XLA Modules:
  0.0 437.9 jit_solution(1056272309662862671)
XLA Ops:
  7.2 0.0 all-gather.4.cloned.1.call-start
  7.2 0.7 all-gather.4.cloned.1.call-update
  7.9 0.0 all-gather.6.cloned.1.call-start
  7.9 0.3 sine_convert_fusion.1
  8.2 0.2 add.80
  8.5 0.7 fusion.82
  9.2 0.7 broadcast_multiply_fusion
  9.8 226.4 %while.13 = (s32[]{:T(128)}, bf16[2,128,16384]{2,1,0:T(8,128)(2,1)}, bf16[2,128,128,128]{3,2,1,0:T(8,128)(2,1)}, bf16[128,256]{1,0:T(8,128)(2,1)S(1)}, bf16[2,12...) while((s32[]{:T(128)}, ...), condition=%wide.region_1.2_spmd.clone.clone, body=%wide.region_0.1_spmd.clone.clone.sunk | while | flops 6754861056 | bytes 285492864 | solution.py:80
  9.8 4.5 %convolution_convert_fusion.3 = bf16[128,128,256]{2,1,0:T(8,128)(2,1)S(1)} fusion(bf16[2,128,128,128]{3,2,1,0:T(8,128)(2,1)} %get-tuple-element.200, s32[]{:T(128)} %get-tuple-element.190, bf16[128,256]{1,0:T(8,128)(2,1)S(1)} %get-tuple-element.201), kind=kOutput, calls=%fused_computation.17.clone.1 | convolution fusion | flops 1077936128 | bytes 12648960 | tf_op jit(solution)/shard_map/while/body/eval_jaxpr/bjk,kv->bjv/dot_general | solution.py:37
  14.4 7.5 %convolution_bitcast_fusion.4 = f32[128,128,256]{1,2,0:T(8,128)} fusion(bf16[128,128,256]{2,1,0:T(8,128)(2,1)S(1)} %convolution_convert_fusion.3), kind=kOutput, calls=%fused_computation.3.clone.1 | convolution fusion | flops 1073987584 | bytes 25165824 | tf_op jit(solution)/shard_map/while/body/eval_jaxpr/uj,bjv->buv/dot_general | solution.py:33
  21.9 7.3 %convolution_bitcast_fusion.5 = f32[128,128,256]{1,2,0:T(8,128)} fusion(bf16[128,128,256]{2,1,0:T(8,128)(2,1)S(1)} %convolution_convert_fusion.3), kind=kOutput, calls=%fused_computation.4.clone.1 | convolution fusion | flops 1073987584 | bytes 25165824 | tf_op jit(solution)/shard_map/while/body/eval_jaxpr/uj,bjv->buv/dot_general | solution.py:33
  29.1 18.8 %fusion.138 = f32[128,128,128]{2,0,1:T(8,128)} fusion(bf16[2,128,64]{1,2,0:T(8,128)(2,1)S(1)} %get-tuple-element.202, s32[]{:T(128)} %get-tuple-element.190, f32[16384]{0:T(1024)S(1)} %get-tuple-element.203, f32[64]{0:T(128)S(1)} %get-tuple-element.204), kind=kOutput, calls=%fused_computation.35.clone.1 | convolution fusion | flops 277872640 | bytes 8471044 | tf_op jit(solution)/shard_map/while/body/eval_jaxpr/dot_general | solution.py:73
  48.0 9.4 %copy.71 = f32[128,128,128]{1,2,0:T(8,128)} copy(f32[128,128,128]{2,0,1:T(8,128)} %fusion.138) | data formatting | bytes 16777216 | tf_op jit(solution)/shard_map/while/body/eval_jaxpr/dot_general | solution.py:73
  57.3 16.7 %fusion.140 = f32[128,128,256]{2,1,0:T(8,128)} fusion(f32[128,128,128]{1,2,0:T(8,128)} %copy.71, f32[128,128,256]{1,2,0:T(8,128)} %convolution_bitcast_fusion.4, f32[128,128,256]{1,2,0:T(8,128)} %convolution_bitcast_fusion.5, bf16[128,256]{1,0:T(8,128)(2,1)S(1)} %get-tuple-element.201), kind=kOutput, calls=%fused_computation.28.clone.1 | convolution fusion | flops 1080033280 | bytes 42008576 | tf_op jit(solution)/shard_map/while/body/eval_jaxpr/bjk,kv->bjv/dot_general | solution.py:37
  74.0 14.0 %fusion.139 = f32[128,128,256]{2,1,0:T(8,128)} fusion(f32[128,128,128]{1,2,0:T(8,128)S(1)} %copy-done, f32[128,128,256]{1,2,0:T(8,128)} %convolution_bitcast_fusion.4, f32[128,128,256]{1,2,0:T(8,128)} %convolution_bitcast_fusion.5, bf16[128,256]{1,0:T(8,128)(2,1)S(1)} %get-tuple-element.201), kind=kOutput, calls=%fused_computation.29.clone.1 | convolution fusion | flops 1082130432 | bytes 42008576 | tf_op jit(solution)/shard_map/while/body/eval_jaxpr/bjk,kv->bjv/dot_general | solution.py:37
  88.0 7.5 %fusion.141 = f32[128,128,128]{2,1,0:T(8,128)S(1)} fusion(f32[128,128,256]{2,1,0:T(8,128)} %fusion.139, f32[128,128,256]{2,1,0:T(8,128)} %fusion.140), kind=kOutput, calls=%fused_computation.30.clone.1 | convolution fusion | flops 541310976 | bytes 25165824 | tf_op jit(solution)/shard_map/while/body/eval_jaxpr/uj,bjv->buv/dot_general | solution.py:33
  95.5 9.7 %multiply_bitcast_fusion.2 = bf16[128,128,128]{1,2,0:T(8,128)(2,1)} fusion(f32[128,128,128]{2,1,0:T(8,128)S(1)} %fusion.141, f32[128,128,256]{2,1,0:T(8,128)} %fusion.139, f32[128,128,256]{2,1,0:T(8,128)} %fusion.140), kind=kOutput, calls=%fused_computation.16.clone.1 | convolution fusion | flops 547602432 | bytes 29360128 | tf_op jit(solution)/shard_map/while/body/eval_jaxpr/uj,bjv->buv/dot_general | solution.py:33
  105.2 7.3 %copy.72 = bf16[128,128,128]{0,2,1:T(8,128)(2,1)} copy(bf16[128,128,128]{1,2,0:T(8,128)(2,1)} %multiply_bitcast_fusion.2) | data formatting | bytes 8388608 | tf_op jit(solution)/shard_map/while/body/eval_jaxpr/div | solution.py:53
  112.5 6.4 %copy.73 = bf16[1,128,16384]{2,1,0:T(8,128)(2,1)} copy(bf16[1,128,16384]{1,2,0:T(8,128)(2,1)} %bitcast.101) | data formatting | bytes 8388608 | tf_op jit(solution)/shard_map/while/body/jit(dynamic_update_index_in_dim)/dynamic_update_slice | solution.py:80
  118.8 4.5 %constant_dynamic-update-slice_fusion.2 = bf16[2,128,16384]{2,1,0:T(8,128)(2,1)} fusion(bf16[2,128,16384]{2,1,0:T(8,128)(2,1)} %get-tuple-element.191, bf16[1,128,16384]{2,1,0:T(8,128)(2,1)} %copy.73, s32[]{:T(128)} %get-tuple-element.190), kind=kLoop, calls=%fused_computation.60.clone.1 | loop fusion | bytes 8389120 | tf_op jit(solution)/shard_map/while/body/jit(dynamic_update_index_in_dim)/dynamic_update_slice | solution.py:80
  123.4 4.5 %convolution_convert_fusion.3 = bf16[128,128,256]{2,1,0:T(8,128)(2,1)S(1)} fusion(bf16[2,128,128,128]{3,2,1,0:T(8,128)(2,1)} %get-tuple-element.200, s32[]{:T(128)} %get-tuple-element.190, bf16[128,256]{1,0:T(8,128)(2,1)S(1)} %get-tuple-element.201), kind=kOutput, calls=%fused_computation.17.clone.1 | convolution fusion | flops 1077936128 | bytes 12648960 | tf_op jit(solution)/shard_map/while/body/eval_jaxpr/bjk,kv->bjv/dot_general | solution.py:37
  127.9 7.3 %convolution_bitcast_fusion.4 = f32[128,128,256]{1,2,0:T(8,128)} fusion(bf16[128,128,256]{2,1,0:T(8,128)(2,1)S(1)} %convolution_convert_fusion.3), kind=kOutput, calls=%fused_computation.3.clone.1 | convolution fusion | flops 1073987584 | bytes 25165824 | tf_op jit(solution)/shard_map/while/body/eval_jaxpr/uj,bjv->buv/dot_general | solution.py:33
  135.1 7.2 %convolution_bitcast_fusion.5 = f32[128,128,256]{1,2,0:T(8,128)} fusion(bf16[128,128,256]{2,1,0:T(8,128)(2,1)S(1)} %convolution_convert_fusion.3), kind=kOutput, calls=%fused_computation.4.clone.1 | convolution fusion | flops 1073987584 | bytes 25165824 | tf_op jit(solution)/shard_map/while/body/eval_jaxpr/uj,bjv->buv/dot_general | solution.py:33
  142.4 18.8 %fusion.138 = f32[128,128,128]{2,0,1:T(8,128)} fusion(bf16[2,128,64]{1,2,0:T(8,128)(2,1)S(1)} %get-tuple-element.202, s32[]{:T(128)} %get-tuple-element.190, f32[16384]{0:T(1024)S(1)} %get-tuple-element.203, f32[64]{0:T(128)S(1)} %get-tuple-element.204), kind=kOutput, calls=%fused_computation.35.clone.1 | convolution fusion | flops 277872640 | bytes 8471044 | tf_op jit(solution)/shard_map/while/body/eval_jaxpr/dot_general | solution.py:73
  161.2 9.3 %copy.71 = f32[128,128,128]{1,2,0:T(8,128)} copy(f32[128,128,128]{2,0,1:T(8,128)} %fusion.138) | data formatting | bytes 16777216 | tf_op jit(solution)/shard_map/while/body/eval_jaxpr/dot_general | solution.py:73
  170.5 16.4 %fusion.140 = f32[128,128,256]{2,1,0:T(8,128)} fusion(f32[128,128,128]{1,2,0:T(8,128)} %copy.71, f32[128,128,256]{1,2,0:T(8,128)} %convolution_bitcast_fusion.4, f32[128,128,256]{1,2,0:T(8,128)} %convolution_bitcast_fusion.5, bf16[128,256]{1,0:T(8,128)(2,1)S(1)} %get-tuple-element.201), kind=kOutput, calls=%fused_computation.28.clone.1 | convolution fusion | flops 1080033280 | bytes 42008576 | tf_op jit(solution)/shard_map/while/body/eval_jaxpr/bjk,kv->bjv/dot_general | solution.py:37
  186.9 14.0 %fusion.139 = f32[128,128,256]{2,1,0:T(8,128)} fusion(f32[128,128,128]{1,2,0:T(8,128)S(1)} %copy-done, f32[128,128,256]{1,2,0:T(8,128)} %convolution_bitcast_fusion.4, f32[128,128,256]{1,2,0:T(8,128)} %convolution_bitcast_fusion.5, bf16[128,256]{1,0:T(8,128)(2,1)S(1)} %get-tuple-element.201), kind=kOutput, calls=%fused_computation.29.clone.1 | convolution fusion | flops 1082130432 | bytes 42008576 | tf_op jit(solution)/shard_map/while/body/eval_jaxpr/bjk,kv->bjv/dot_general | solution.py:37
  200.9 7.5 %fusion.141 = f32[128,128,128]{2,1,0:T(8,128)S(1)} fusion(f32[128,128,256]{2,1,0:T(8,128)} %fusion.139, f32[128,128,256]{2,1,0:T(8,128)} %fusion.140), kind=kOutput, calls=%fused_computation.30.clone.1 | convolution fusion | flops 541310976 | bytes 25165824 | tf_op jit(solution)/shard_map/while/body/eval_jaxpr/uj,bjv->buv/dot_general | solution.py:33
  208.4 9.7 %multiply_bitcast_fusion.2 = bf16[128,128,128]{1,2,0:T(8,128)(2,1)} fusion(f32[128,128,128]{2,1,0:T(8,128)S(1)} %fusion.141, f32[128,128,256]{2,1,0:T(8,128)} %fusion.139, f32[128,128,256]{2,1,0:T(8,128)} %fusion.140), kind=kOutput, calls=%fused_computation.16.clone.1 | convolution fusion | flops 547602432 | bytes 29360128 | tf_op jit(solution)/shard_map/while/body/eval_jaxpr/uj,bjv->buv/dot_general | solution.py:33
  218.1 7.3 %copy.72 = bf16[128,128,128]{0,2,1:T(8,128)(2,1)} copy(bf16[128,128,128]{1,2,0:T(8,128)(2,1)} %multiply_bitcast_fusion.2) | data formatting | bytes 8388608 | tf_op jit(solution)/shard_map/while/body/eval_jaxpr/div | solution.py:53
  225.3 6.4 %copy.73 = bf16[1,128,16384]{2,1,0:T(8,128)(2,1)} copy(bf16[1,128,16384]{1,2,0:T(8,128)(2,1)} %bitcast.101) | data formatting | bytes 8388608 | tf_op jit(solution)/shard_map/while/body/jit(dynamic_update_index_in_dim)/dynamic_update_slice | solution.py:80
  231.7 4.5 %constant_dynamic-update-slice_fusion.2 = bf16[2,128,16384]{2,1,0:T(8,128)(2,1)} fusion(bf16[2,128,16384]{2,1,0:T(8,128)(2,1)} %get-tuple-element.191, bf16[1,128,16384]{2,1,0:T(8,128)(2,1)} %copy.73, s32[]{:T(128)} %get-tuple-element.190), kind=kLoop, calls=%fused_computation.60.clone.1 | loop fusion | bytes 8389120 | tf_op jit(solution)/shard_map/while/body/jit(dynamic_update_index_in_dim)/dynamic_update_slice | solution.py:80
  236.9 8.6 %fusion.72 = bf16[256,16384]{1,0:T(8,128)(2,1)} fusion(bf16[2,128,16384]{2,1,0:T(8,128)(2,1)} %get-tuple-element.79, pred[256]{0:T(512)(128)(4,1)S(1)} %iota_compare_fusion.3), kind=kLoop, calls=%fused_computation.76 | loop fusion | flops 4194304 | bytes 16777472 | tf_op jit(solution)/shard_map/convert_element_type | solution.py:89
  245.4 6.9 %fusion.86 = f32[256,128]{1,0:T(8,128)S(1)} fusion(bf16[256,16384]{1,0:T(8,128)(2,1)} %fusion.72, bf16[16384,128]{1,0:T(8,128)(2,1)} %all-gather.4.cloned.1.call-done), kind=kOutput, calls=%fused_computation.108 | convolution fusion | flops 1073741824 | bytes 12713984 | tf_op jit(solution)/shard_map/dot_general | solution.py:91
  252.4 1.0 fusion.87
  253.4 0.0 all-gather.6.cloned.1.call-update
  253.4 0.0 reduce-scatter.2.cloned.1.call-start
  253.4 40.6 %all-gather.6.cloned.1.call-done = f32[2048,128]{1,0:T(8,128)} async-done(((f32[128,128]{1,0:T(8,128)}), f32[2048,128]{1,0:T(8,128)}) %all-gather.6.cloned.1.call-update) | async-done | bytes 1048592 | tf_op jit(solution)/shard_map/all_gather | solution.py:97
  294.0 1.3 reduce_sum.9
  295.3 0.1 copy.50
  295.4 11.7 %cholesky.16 = f32[128,128]{1,0:T(8,128)S(1)} custom-call(f32[128,128]{1,0:T(8,128)S(1)} %fusion.78), custom_call_target="Cholesky" | custom-call | tf_op jit(solution)/shard_map/jit(cholesky)/cholesky | solution.py:97
  307.1 0.6 compare_reduce_fusion
  307.8 0.7 fusion.73
  308.5 9.8 %custom-call.6 = f32[1,128,128]{1,2,0:T(8,128)S(1)} custom-call(f32[1,128,128]{2,1,0:T(8,128)S(1)} %fusion.73), custom_call_target="InvertDiagBlocksLowerTriangular" | custom-call | tf_op jit(solution)/shard_map/triangular_solve | solution.py:98
  318.3 0.3 convolution_convert_fusion.1
  318.6 9.0 %fusion.88 = f32[16384,128]{1,0:T(8,128)} fusion(bf16[256,16384]{1,0:T(8,128)(2,1)} %fusion.72, bf16[256,128]{1,0:T(8,128)(2,1)S(1)} %convolution_convert_fusion.1), kind=kOutput, calls=%fused_computation.110 | convolution fusion | flops 1073741824 | bytes 16842752 | tf_op jit(solution)/shard_map/dot_general | solution.py:103
  327.6 0.0 reduce-scatter.2.cloned.1.call-update
  327.6 103.7 %reduce-scatter.2.cloned.1.call-done = f32[1024,128]{1,0:T(8,128)} async-done(((f32[16384,128]{1,0:T(8,128)}), f32[1024,128]{1,0:T(8,128)}) %reduce-scatter.2.cloned.1.call-update) | async-done | bytes 524304 | tf_op jit(solution)/shard_map/reduce_scatter | solution.py:102
  (14 shorter events, 0.1 us)
Async XLA Ops:
  7.2 238.3 %all-gather.4.cloned.1.call-start = ((), (), s32[]{:S(2)}) async-start(), calls=%async_computation.1 | async-start | bytes 4456448 | tf_op jit(solution)/shard_map/all_gather | solution.py:93
  7.9 286.1 %all-gather.6.cloned.1.call-start = ((), (), s32[]{:S(2)}) async-start(), calls=%async_computation.3 | async-start | bytes 1114112 | tf_op jit(solution)/shard_map/all_gather | solution.py:97
  57.3 16.7 %copy-start = (f32[128,128,128]{1,2,0:T(8,128)S(1)}, f32[128,128,128]{1,2,0:T(8,128)}, u32[]{:S(2)}) copy-start(f32[128,128,128]{1,2,0:T(8,128)} %copy.71) | copy-start | bytes 25165828 | tf_op jit(solution)/shard_map/while
  170.5 16.4 %copy-start = (f32[128,128,128]{1,2,0:T(8,128)S(1)}, f32[128,128,128]{1,2,0:T(8,128)}, u32[]{:S(2)}) copy-start(f32[128,128,128]{1,2,0:T(8,128)} %copy.71) | copy-start | bytes 25165828 | tf_op jit(solution)/shard_map/while
  253.4 177.9 %reduce-scatter.2.cloned.1.call-start = ((), (), s32[]{:S(2)}) async-start(), calls=%async_computation.2 | async-start | bytes 8912896 | tf_op jit(solution)/shard_map/reduce_scatter | solution.py:102
  318.5 9.0 %copy-start.1 = (bf16[256,128]{1,0:T(8,128)(2,1)}, bf16[256,128]{1,0:T(8,128)(2,1)S(1)}, u32[]{:S(2)}) copy-start(bf16[256,128]{1,0:T(8,128)(2,1)S(1)} %convolution_convert_fusion.1) | copy-start | bytes 196612
Sparse Core Ops, SparseCore 0:
  10.2 53.3 all-gather.3
  253.5 40.4 all-gather.5
  327.7 103.5 reduce-scatter.1
